TPU v7x, 32 devices: a whole 2x2x4 slice. The times are simulated.
32 devices in a mesh: band: 16 (over z, x, core), head: 2 (over y).
Axes of the slice: x: 2, y: 2, z: 4, core: 2. Of those that a mesh axis runs over, the one named last changes fastest.
Arguments:
- queries: bfloat16 [16, 3, 16, 512], P('band', None, None, 'head'), may hold values from -16 to 16
- attn_keys: bfloat16 [16, 3, 16, 512], P('band', None, None, 'head'), may hold values from -16 to 16
- attn_values: bfloat16 [16, 3, 16, 512], P('band', None, None, 'head'), may hold values from -16 to 16
- out_proj: bfloat16 [512, 1024], P('head'), may hold values from -0.25 to 0.25
- grad_out: bfloat16 [16, 3, 16, 1024], P('band', None, 'head'), may hold values from -24 to 24
- plane_axes: int32 [3, 2], replicated, may hold values from 0 to 2, as said below
Outputs:
- layer_out: bfloat16 [16, 3, 16, 1024], P('band', None, 'head')
- grad_queries: bfloat16 [16, 3, 16, 512], P('band', None, None, 'head')
- grad_keys: bfloat16 [16, 3, 16, 512], P('band', None, None, 'head')
- grad_values: bfloat16 [16, 3, 16, 512], P('band', None, None, 'head')
Inputs may be any that keep to these rules, and one draw needn't show every extreme that they name: `plane_axes`: row p holds plane p's row axis and then its column axis, two different world axes; the three planes lack three different world axes.
All inputs are finite; a program needn't handle non-finite values.
Results may differ from a plain program's by a relative error of at most 0.018.
Values may be sent and summed in bfloat16 or wider, within the bound.
A program may use at most 64 MiB of HBM per device.

v0:
```python
import jax
import jax.numpy as jnp
from jax import lax
from jax.sharding import PartitionSpec as P

HEAD_DIM = 64


def partner_blocks(plane_axes):
    axis_of = jnp.concatenate([plane_axes[:, 0], plane_axes[:, 1]])
    blocks = jnp.arange(6, dtype=jnp.int32)
    same = (axis_of[:, None] == axis_of[None, :]) & (blocks[:, None] != blocks[None, :])
    return jnp.sum(jnp.where(same, blocks[None, :], 0), axis=1)


def by_head(values):
    return values.reshape(values.shape[:-1] + (values.shape[-1] // HEAD_DIM, HEAD_DIM))


def flatten(values):
    return values.reshape(values.shape[:2] + (-1,))


def log_total(scores):
    top = jnp.max(scores, axis=-1, keepdims=True)
    return top[..., 0] + jnp.log(jnp.sum(jnp.exp(scores - top), axis=-1))


def line_scores(query_line, key_line, partner):
    factor = HEAD_DIM ** (-0.5)
    query_heads = by_head(query_line)
    key_heads = by_head(key_line)
    partner_keys = jnp.take(key_heads, partner, axis=0)
    cross = (
        jnp.einsum("bahe,bche->bhac", query_heads, partner_keys, preferred_element_type=jnp.float32)
        * factor
    )
    own = (
        jnp.einsum(
            "bahe,bche->bhac", query_heads[:3], key_heads[:3], preferred_element_type=jnp.float32
        )
        * factor
    )
    return (own, cross)


def forward_core(own, cross, value_line, partner):
    value_heads = by_head(value_line)
    partner_values = jnp.take(value_heads, partner, axis=0)
    length = own.shape[-1]
    near_scores = jnp.concatenate([own, cross[:3]], axis=-1)
    near_total = log_total(near_scores)
    near_prob = jnp.exp(near_scores - near_total[..., None]).astype(jnp.bfloat16)
    near_out = jnp.einsum(
        "bhac,bche->bahe",
        near_prob[..., :length],
        value_heads[:3],
        preferred_element_type=jnp.float32,
    )
    near_out = near_out + jnp.einsum(
        "bhac,bche->bahe",
        near_prob[..., length:],
        partner_values[:3],
        preferred_element_type=jnp.float32,
    )
    far_total = log_total(cross[3:])
    far_prob = jnp.exp(cross[3:] - far_total[..., None]).astype(jnp.bfloat16)
    far_out = jnp.einsum(
        "bhac,bche->bahe", far_prob, partner_values[3:], preferred_element_type=jnp.float32
    )
    return (
        jnp.transpose(near_total, (0, 2, 1)),
        flatten(near_out),
        jnp.transpose(far_total, (0, 2, 1)),
        flatten(far_out),
    )


def backward_core(own, cross, line, partner):
    factor = HEAD_DIM ** (-0.5)
    query_line, key_line, value_line, grad_line, total_line, delta_line = line
    query_heads = by_head(query_line)
    key_heads = by_head(key_line)
    value_heads = by_head(value_line)
    grad_heads = by_head(grad_line)
    partner_keys = jnp.take(key_heads, partner, axis=0)
    partner_values = jnp.take(value_heads, partner, axis=0)
    total = jnp.transpose(total_line, (0, 2, 1))[..., None]
    delta = jnp.transpose(delta_line, (0, 2, 1))[..., None]
    cross_prob = jnp.exp(cross - total).astype(jnp.bfloat16)
    own_prob = jnp.exp(own - total[:3]).astype(jnp.bfloat16)
    cross_grad = jnp.einsum(
        "bahe,bche->bhac", grad_heads, partner_values, preferred_element_type=jnp.float32
    )
    own_grad = jnp.einsum(
        "bahe,bche->bhac", grad_heads[:3], value_heads[:3], preferred_element_type=jnp.float32
    )
    cross_step = (cross_prob.astype(jnp.float32) * (cross_grad - delta) * factor).astype(
        jnp.bfloat16
    )
    own_step = (own_prob.astype(jnp.float32) * (own_grad - delta[:3]) * factor).astype(jnp.bfloat16)
    grad_query = jnp.einsum(
        "bhac,bche->bahe", cross_step, partner_keys, preferred_element_type=jnp.float32
    )
    grad_query = grad_query.at[:3].add(
        jnp.einsum("bhac,bche->bahe", own_step, key_heads[:3], preferred_element_type=jnp.float32)
    )
    toward_keys = jnp.einsum(
        "bhac,bahe->bche", cross_step, query_heads, preferred_element_type=jnp.float32
    )
    toward_values = jnp.einsum(
        "bhac,bahe->bche", cross_prob, grad_heads, preferred_element_type=jnp.float32
    )
    grad_key = jnp.take(toward_keys, partner, axis=0)
    grad_key = grad_key.at[:3].add(
        jnp.einsum("bhac,bahe->bche", own_step, query_heads[:3], preferred_element_type=jnp.float32)
    )
    grad_value = jnp.take(toward_values, partner, axis=0)
    grad_value = grad_value.at[:3].add(
        jnp.einsum("bhac,bahe->bche", own_prob, grad_heads[:3], preferred_element_type=jnp.float32)
    )
    return (flatten(grad_query), flatten(grad_key), flatten(grad_value))


def to_columns(values):
    return jnp.transpose(values, (2, 1, 0, 3))


def body(queries, attn_keys, attn_values, out_proj, grad_out, plane_axes):
    partner = partner_blocks(plane_axes)
    column_q, column_k, column_v = (
        lax.all_to_all(to_columns(queries), "band", split_axis=0, concat_axis=2, tiled=True),
        lax.all_to_all(to_columns(attn_keys), "band", split_axis=0, concat_axis=2, tiled=True),
        lax.all_to_all(to_columns(attn_values), "band", split_axis=0, concat_axis=2, tiled=True),
    )
    query_lines = jnp.concatenate([queries, column_q], axis=1)
    key_lines = jnp.concatenate([attn_keys, column_k], axis=1)
    value_lines = jnp.concatenate([attn_values, column_v], axis=1)
    lines = (query_lines, key_lines, value_lines)

    def forward_fresh(line):
        own, cross = line_scores(line[0], line[1], partner)
        return forward_core(own, cross, line[2], partner)

    near_total, near_out, far_total, far_out = lax.map(forward_fresh, lines)
    far_back, far_total_back = (
        lax.all_to_all(far_out, "band", split_axis=2, concat_axis=0, tiled=True),
        lax.all_to_all(far_total, "band", split_axis=2, concat_axis=0, tiled=True),
    )
    far_out = to_columns(far_back)
    far_total = to_columns(far_total_back)
    top = jnp.maximum(near_total, far_total)
    log_all = top + jnp.log(jnp.exp(near_total - top) + jnp.exp(far_total - top))
    attended = (
        by_head(near_out) * jnp.exp(near_total - log_all)[..., None]
        + by_head(far_out) * jnp.exp(far_total - log_all)[..., None]
    )
    attended = attended.reshape(queries.shape).astype(jnp.bfloat16)
    summed = lax.psum_scatter(
        jnp.einsum("ipjf,fd->jipd", attended, out_proj, preferred_element_type=jnp.float32).astype(
            jnp.bfloat16
        ),
        "head",
        scatter_dimension=0,
        tiled=True,
    ).astype(jnp.float32)
    layer_out = jnp.transpose(summed, (1, 2, 0, 3)).astype(jnp.bfloat16)
    grad_attended = jnp.einsum(
        "ipjd,fd->ipjf",
        lax.all_gather(grad_out, "head", axis=2, tiled=True),
        out_proj,
        preferred_element_type=jnp.float32,
    ).astype(jnp.bfloat16)
    delta = jnp.sum(
        by_head(grad_attended).astype(jnp.float32) * by_head(attended).astype(jnp.float32), axis=-1
    )
    grad_column, total_column, delta_column = (
        lax.all_to_all(
            to_columns(grad_attended.astype(jnp.float32)),
            "band",
            split_axis=0,
            concat_axis=2,
            tiled=True,
        ),
        lax.all_to_all(to_columns(log_all), "band", split_axis=0, concat_axis=2, tiled=True),
        lax.all_to_all(to_columns(delta), "band", split_axis=0, concat_axis=2, tiled=True),
    )
    grad_lines = jnp.concatenate([grad_attended, grad_column.astype(jnp.bfloat16)], axis=1)
    total_lines = jnp.concatenate([log_all, total_column], axis=1)
    delta_lines = jnp.concatenate([delta, delta_column], axis=1)
    back_lines = (query_lines, key_lines, value_lines, grad_lines, total_lines, delta_lines)

    def backward_fresh(line):
        own, cross = line_scores(line[0], line[1], partner)
        return backward_core(own, cross, line, partner)

    grad_q, grad_k, grad_v = lax.map(backward_fresh, back_lines)
    back_q, back_k, back_v = (
        lax.all_to_all(
            grad_q[:, 3:].astype(jnp.bfloat16), "band", split_axis=2, concat_axis=0, tiled=True
        ).astype(jnp.float32),
        lax.all_to_all(
            grad_k[:, 3:].astype(jnp.bfloat16), "band", split_axis=2, concat_axis=0, tiled=True
        ).astype(jnp.float32),
        lax.all_to_all(
            grad_v[:, 3:].astype(jnp.bfloat16), "band", split_axis=2, concat_axis=0, tiled=True
        ).astype(jnp.float32),
    )
    grad_queries = (grad_q[:, :3] + to_columns(back_q)).astype(jnp.bfloat16)
    grad_keys = (grad_k[:, :3] + to_columns(back_k)).astype(jnp.bfloat16)
    grad_values = (grad_v[:, :3] + to_columns(back_v)).astype(jnp.bfloat16)
    return (layer_out, grad_queries, grad_keys, grad_values)


def solution(mesh):
    in_specs = (
        P("band", None, None, "head"),
        P("band", None, None, "head"),
        P("band", None, None, "head"),
        P("head", None),
        P("band", None, "head", None),
        P(),
    )
    out_specs = (
        P("band", None, "head", None),
        P("band", None, None, "head"),
        P("band", None, None, "head"),
        P("band", None, None, "head"),
    )
    return jax.shard_map(body, mesh=mesh, in_specs=in_specs, out_specs=out_specs, check_vma=False)
```

profile of v0, /device:TPU:0, one launch (start us, length us, event | category | flops | bytes accessed | tf_op | source)
XLA Modules:
  0.0 142.3 jit_solution(6073546607036354526)
XLA Ops:
  7.2 1.4 %copy.319 = bf16[1,3,16,256]{3,1,0,2:T(4,128)(2,1)} copy(bf16[1,3,16,256]{3,2,1,0:T(8,128)(2,1)} %param.18) | data formatting | bytes 49152 | tf_op args[2]
  8.6 7.4 %all-to-all-start.2 = ((bf16[16,3,1,256]{3,1,2,0:T(4,128)(2,1)}), bf16[16,3,1,256]{3,1,2,0:T(4,128)(2,1)S(1)}, u32[]{:S(2)}, u32[]{:S(2)}) async-start(bf16[16,3,1,256]{3,1,2,0:T(4,128)(2,1)} %bitcast.215), calls=%async_computation.2 | async-start | bytes 65536 | tf_op jit(solution)/shard_map/all_to_all | solution.py:134
  16.0 4.8 %all_gather.3 = bf16[1,3,16,1024]{3,2,1,0:T(8,128)(2,1)S(1)} all-gather(bf16[1,3,8,1024]{3,2,1,0:T(8,128)(2,1)S(1)} %copy-done.4), channel_id=1, replica_groups=mesh['band'=16,'head'=2] {'head'}, dimensions={2}, use_global_device_ids=true | all-gather | bytes 147456 | tf_op jit(solution)/shard_map/all_gather | solution.py:170
  23.8 6.0 %all-to-all-start.1 = ((bf16[16,3,1,256]{3,1,2,0:T(4,128)(2,1)}), bf16[16,3,1,256]{3,1,2,0:T(4,128)(2,1)S(1)}, u32[]{:S(2)}, u32[]{:S(2)}) async-start(bf16[16,3,1,256]{3,1,2,0:T(4,128)(2,1)} %bitcast.216), calls=%async_computation.1 | async-start | bytes 65536 | tf_op jit(solution)/shard_map/all_to_all | solution.py:133
  29.8 0.6 copy.321
  31.2 0.7 reduce.15
  31.9 0.6 reshape.406
  32.6 3.8 %all-to-all-done.1 = bf16[16,3,1,256]{3,1,2,0:T(4,128)(2,1)S(1)} async-done(((bf16[16,3,1,256]{3,1,2,0:T(4,128)(2,1)}), bf16[16,3,1,256]{3,1,2,0:T(4,128)(2,1)S(1)}, u32[]{:S(2)}, u32[]{:S(2)}) %all-to-all-start.1) | async-done | bytes 24608 | tf_op jit(solution)/shard_map/all_to_all | solution.py:133
  36.4 3.5 %all-to-all-start = ((bf16[16,3,1,256]{3,1,2,0:T(4,128)(2,1)}), bf16[16,3,1,256]{3,1,2,0:T(4,128)(2,1)S(1)}, u32[]{:S(2)}, u32[]{:S(2)}) async-start(bf16[16,3,1,256]{3,1,2,0:T(4,128)(2,1)} %bitcast.217), calls=%async_computation | async-start | bytes 65536 | tf_op jit(solution)/shard_map/all_to_all | solution.py:132
  40.1 6.4 %all-to-all-done = bf16[16,3,1,256]{3,1,2,0:T(4,128)(2,1)S(1)} async-done(((bf16[16,3,1,256]{3,1,2,0:T(4,128)(2,1)}), bf16[16,3,1,256]{3,1,2,0:T(4,128)(2,1)S(1)}, u32[]{:S(2)}, u32[]{:S(2)}) %all-to-all-start) | async-done | bytes 24608 | tf_op jit(solution)/shard_map/all_to_all | solution.py:132
  46.5 3.5 %all-to-all-start.6 = ((bf16[16,2,384]{2,1,0:T(2,128)(2,1)}), bf16[16,2,384]{2,1,0:T(2,128)(2,1)S(1)}, u32[]{:S(2)}, u32[]{:S(2)}) async-start(bf16[16,2,384]{2,1,0:T(2,128)(2,1)} %reshape.406), calls=%async_computation.6 | async-start | bytes 49152 | tf_op jit(solution)/shard_map/all_to_all | solution.py:178
  51.3 5.3 %all-to-all-done.6 = bf16[16,2,384]{2,1,0:T(2,128)(2,1)S(1)} async-done(((bf16[16,2,384]{2,1,0:T(2,128)(2,1)}), bf16[16,2,384]{2,1,0:T(2,128)(2,1)S(1)}, u32[]{:S(2)}, u32[]{:S(2)}) %all-to-all-start.6) | async-done | bytes 24608 | tf_op jit(solution)/shard_map/all_to_all | solution.py:178
  57.4 0.7 copy.231
  58.1 3.5 %all-to-all-start.3 = ((f32[1,3,16,4]{3,0,1,2:T(1,128)}), f32[1,3,16,4]{3,0,1,2:T(1,128)S(1)}, u32[]{:S(2)}, u32[]{:S(2)}) async-start(f32[1,3,16,4]{3,0,1,2:T(1,128)} %copy.231), calls=%async_computation.3 | async-start | bytes 49152 | tf_op jit(solution)/shard_map/all_to_all | solution.py:148
  62.2 0.7 reshape.401
  62.9 5.3 %all-to-all-done.3 = f32[1,3,16,4]{3,0,1,2:T(1,128)S(1)} async-done(((f32[1,3,16,4]{3,0,1,2:T(1,128)}), f32[1,3,16,4]{3,0,1,2:T(1,128)S(1)}, u32[]{:S(2)}, u32[]{:S(2)}) %all-to-all-start.3) | async-done | bytes 800 | tf_op jit(solution)/shard_map/all_to_all | solution.py:148
  68.4 0.7 copy.238
  69.1 3.5 %all-to-all-start.5 = ((f32[16,3,1,4]{3,2,1,0:T(1,128)}), f32[16,3,1,4]{3,2,1,0:T(1,128)S(1)}, u32[]{:S(2)}, u32[]{:S(2)}) async-start(f32[16,3,1,4]{3,2,1,0:T(1,128)} %copy.238), calls=%async_computation.5 | async-start | bytes 49152 | tf_op jit(solution)/shard_map/all_to_all | solution.py:185
  72.8 6.4 %all-to-all-done.5 = f32[16,3,1,4]{3,2,1,0:T(1,128)S(1)} async-done(((f32[16,3,1,4]{3,2,1,0:T(1,128)}), f32[16,3,1,4]{3,2,1,0:T(1,128)S(1)}, u32[]{:S(2)}, u32[]{:S(2)}) %all-to-all-start.5) | async-done | bytes 800 | tf_op jit(solution)/shard_map/all_to_all | solution.py:185
  79.2 3.5 %all-to-all-start.4 = ((f32[1,3,16,256]{3,0,1,2:T(1,128)}), f32[1,3,16,256]{3,0,1,2:T(1,128)S(1)}, u32[]{:S(2)}, u32[]{:S(2)}) async-start(f32[1,3,16,256]{3,0,1,2:T(1,128)} %reshape.401), calls=%async_computation.4 | async-start | bytes 98304 | tf_op jit(solution)/shard_map/all_to_all | solution.py:147
  82.8 6.6 %all-to-all-done.4 = f32[1,3,16,256]{3,0,1,2:T(1,128)S(1)} async-done(((f32[1,3,16,256]{3,0,1,2:T(1,128)}), f32[1,3,16,256]{3,0,1,2:T(1,128)S(1)}, u32[]{:S(2)}, u32[]{:S(2)}) %all-to-all-start.4) | async-done | bytes 49184 | tf_op jit(solution)/shard_map/all_to_all | solution.py:147
  90.1 0.7 copy.245
  90.8 3.5 %all-to-all-start.7 = ((f32[16,3,1,4]{3,2,1,0:T(1,128)}), f32[16,3,1,4]{3,2,1,0:T(1,128)S(1)}, u32[]{:S(2)}, u32[]{:S(2)}) async-start(f32[16,3,1,4]{3,2,1,0:T(1,128)} %copy.245), calls=%async_computation.7 | async-start | bytes 49152 | tf_op jit(solution)/shard_map/all_to_all | solution.py:186
  94.7 0.7 copy.281
  95.4 5.5 %all-to-all-done.7 = f32[16,3,1,4]{3,2,1,0:T(1,128)S(1)} async-done(((f32[16,3,1,4]{3,2,1,0:T(1,128)}), f32[16,3,1,4]{3,2,1,0:T(1,128)S(1)}, u32[]{:S(2)}, u32[]{:S(2)}) %all-to-all-start.7) | async-done | bytes 800 | tf_op jit(solution)/shard_map/all_to_all | solution.py:186
  103.9 0.6 copy.263
  104.6 3.5 %all-to-all-start.10 = ((bf16[1,3,16,256]{3,1,0,2:T(4,128)(2,1)}), bf16[1,3,16,256]{3,1,0,2:T(4,128)(2,1)S(1)}, u32[]{:S(2)}, u32[]{:S(2)}) async-start(bf16[1,3,16,256]{3,1,0,2:T(4,128)(2,1)} %copy.263), calls=%async_computation.10 | async-start | bytes 65536 | tf_op jit(solution)/shard_map/all_to_all | solution.py:205
  110.2 4.4 %all-to-all-done.10 = bf16[1,3,16,256]{3,1,0,2:T(4,128)(2,1)S(1)} async-done(((bf16[1,3,16,256]{3,1,0,2:T(4,128)(2,1)}), bf16[1,3,16,256]{3,1,0,2:T(4,128)(2,1)S(1)}, u32[]{:S(2)}, u32[]{:S(2)}) %all-to-all-start.10) | async-done | bytes 24608 | tf_op jit(solution)/shard_map/all_to_all | solution.py:205
  114.7 3.5 %all-to-all-start.9 = ((bf16[1,3,16,256]{3,1,0,2:T(4,128)(2,1)}), bf16[1,3,16,256]{3,1,0,2:T(4,128)(2,1)S(1)}, u32[]{:S(2)}, u32[]{:S(2)}) async-start(bf16[1,3,16,256]{3,1,0,2:T(4,128)(2,1)} %copy.257), calls=%async_computation.9 | async-start | bytes 65536 | tf_op jit(solution)/shard_map/all_to_all | solution.py:202
  118.8 6.0 %all-to-all-done.9 = bf16[1,3,16,256]{3,1,0,2:T(4,128)(2,1)S(1)} async-done(((bf16[1,3,16,256]{3,1,0,2:T(4,128)(2,1)}), bf16[1,3,16,256]{3,1,0,2:T(4,128)(2,1)S(1)}, u32[]{:S(2)}, u32[]{:S(2)}) %all-to-all-start.9) | async-done | bytes 24608 | tf_op jit(solution)/shard_map/all_to_all | solution.py:202
  124.8 3.5 %all-to-all-start.8 = ((bf16[1,3,16,256]{3,1,0,2:T(4,128)(2,1)}), bf16[1,3,16,256]{3,1,0,2:T(4,128)(2,1)S(1)}, u32[]{:S(2)}, u32[]{:S(2)}) async-start(bf16[1,3,16,256]{3,1,0,2:T(4,128)(2,1)} %copy.251), calls=%async_computation.8 | async-start | bytes 65536 | tf_op jit(solution)/shard_map/all_to_all | solution.py:199
  128.9 6.0 %all-to-all-done.8 = bf16[1,3,16,256]{3,1,0,2:T(4,128)(2,1)S(1)} async-done(((bf16[1,3,16,256]{3,1,0,2:T(4,128)(2,1)}), bf16[1,3,16,256]{3,1,0,2:T(4,128)(2,1)S(1)}, u32[]{:S(2)}, u32[]{:S(2)}) %all-to-all-start.8) | async-done | bytes 24608 | tf_op jit(solution)/shard_map/all_to_all | solution.py:199
  (102 shorter events, 15.0 us)
Async XLA Ops:
  7.2 13.6 %copy-start = (bf16[256,1024]{1,0:T(8,128)(2,1)S(1)}, bf16[256,1024]{1,0:T(8,128)(2,1)}, u32[]{:S(2)}) copy-start(bf16[256,1024]{1,0:T(8,128)(2,1)} %param.19) | copy-start | bytes 1572868
  7.2 8.8 %copy-start.4 = (bf16[1,3,8,1024]{3,2,1,0:T(8,128)(2,1)S(1)}, bf16[1,3,8,1024]{3,2,1,0:T(8,128)(2,1)}, u32[]{:S(2)}) copy-start(bf16[1,3,8,1024]{3,2,1,0:T(8,128)(2,1)} %param.20) | copy-start | bytes 147460
  8.6 15.2 %all-to-all-start.2 = ((bf16[16,3,1,256]{3,1,2,0:T(4,128)(2,1)}), bf16[16,3,1,256]{3,1,2,0:T(4,128)(2,1)S(1)}, u32[]{:S(2)}, u32[]{:S(2)}) async-start(bf16[16,3,1,256]{3,1,2,0:T(4,128)(2,1)} %bitcast.215), calls=%async_computation.2 | async-start | bytes 65536 | tf_op jit(solution)/shard_map/all_to_all | solution.py:134
  21.1 0.7 copy-start.5
  21.1 1.0 copy-start.2
  22.0 0.7 copy-start.1
  23.8 12.6 %all-to-all-start.1 = ((bf16[16,3,1,256]{3,1,2,0:T(4,128)(2,1)}), bf16[16,3,1,256]{3,1,2,0:T(4,128)(2,1)S(1)}, u32[]{:S(2)}, u32[]{:S(2)}) async-start(bf16[16,3,1,256]{3,1,2,0:T(4,128)(2,1)} %bitcast.216), calls=%async_computation.1 | async-start | bytes 65536 | tf_op jit(solution)/shard_map/all_to_all | solution.py:133
  29.8 0.7 copy-start.3
  36.4 10.1 %all-to-all-start = ((bf16[16,3,1,256]{3,1,2,0:T(4,128)(2,1)}), bf16[16,3,1,256]{3,1,2,0:T(4,128)(2,1)S(1)}, u32[]{:S(2)}, u32[]{:S(2)}) async-start(bf16[16,3,1,256]{3,1,2,0:T(4,128)(2,1)} %bitcast.217), calls=%async_computation | async-start | bytes 65536 | tf_op jit(solution)/shard_map/all_to_all | solution.py:132
  46.5 10.0 %all-to-all-start.6 = ((bf16[16,2,384]{2,1,0:T(2,128)(2,1)}), bf16[16,2,384]{2,1,0:T(2,128)(2,1)S(1)}, u32[]{:S(2)}, u32[]{:S(2)}) async-start(bf16[16,2,384]{2,1,0:T(2,128)(2,1)} %reshape.406), calls=%async_computation.6 | async-start | bytes 49152 | tf_op jit(solution)/shard_map/all_to_all | solution.py:178
  58.1 10.0 %all-to-all-start.3 = ((f32[1,3,16,4]{3,0,1,2:T(1,128)}), f32[1,3,16,4]{3,0,1,2:T(1,128)S(1)}, u32[]{:S(2)}, u32[]{:S(2)}) async-start(f32[1,3,16,4]{3,0,1,2:T(1,128)} %copy.231), calls=%async_computation.3 | async-start | bytes 49152 | tf_op jit(solution)/shard_map/all_to_all | solution.py:148
  69.1 10.0 %all-to-all-start.5 = ((f32[16,3,1,4]{3,2,1,0:T(1,128)}), f32[16,3,1,4]{3,2,1,0:T(1,128)S(1)}, u32[]{:S(2)}, u32[]{:S(2)}) async-start(f32[16,3,1,4]{3,2,1,0:T(1,128)} %copy.238), calls=%async_computation.5 | async-start | bytes 49152 | tf_op jit(solution)/shard_map/all_to_all | solution.py:185
  79.2 10.2 %all-to-all-start.4 = ((f32[1,3,16,256]{3,0,1,2:T(1,128)}), f32[1,3,16,256]{3,0,1,2:T(1,128)S(1)}, u32[]{:S(2)}, u32[]{:S(2)}) async-start(f32[1,3,16,256]{3,0,1,2:T(1,128)} %reshape.401), calls=%async_computation.4 | async-start | bytes 98304 | tf_op jit(solution)/shard_map/all_to_all | solution.py:147
  90.8 10.0 %all-to-all-start.7 = ((f32[16,3,1,4]{3,2,1,0:T(1,128)}), f32[16,3,1,4]{3,2,1,0:T(1,128)S(1)}, u32[]{:S(2)}, u32[]{:S(2)}) async-start(f32[16,3,1,4]{3,2,1,0:T(1,128)} %copy.245), calls=%async_computation.7 | async-start | bytes 49152 | tf_op jit(solution)/shard_map/all_to_all | solution.py:186
  94.3 41.2 %reduce-scatter.4.cloned.1.call-start = ((), (), s32[]{:S(2)}) async-start(), calls=%async_computation.12 | async-start | bytes 147456
  104.6 10.1 %all-to-all-start.10 = ((bf16[1,3,16,256]{3,1,0,2:T(4,128)(2,1)}), bf16[1,3,16,256]{3,1,0,2:T(4,128)(2,1)S(1)}, u32[]{:S(2)}, u32[]{:S(2)}) async-start(bf16[1,3,16,256]{3,1,0,2:T(4,128)(2,1)} %copy.263), calls=%async_computation.10 | async-start | bytes 65536 | tf_op jit(solution)/shard_map/all_to_all | solution.py:205
  114.7 10.1 %all-to-all-start.9 = ((bf16[1,3,16,256]{3,1,0,2:T(4,128)(2,1)}), bf16[1,3,16,256]{3,1,0,2:T(4,128)(2,1)S(1)}, u32[]{:S(2)}, u32[]{:S(2)}) async-start(bf16[1,3,16,256]{3,1,0,2:T(4,128)(2,1)} %copy.257), calls=%async_computation.9 | async-start | bytes 65536 | tf_op jit(solution)/shard_map/all_to_all | solution.py:202
  124.8 10.1 %all-to-all-start.8 = ((bf16[1,3,16,256]{3,1,0,2:T(4,128)(2,1)}), bf16[1,3,16,256]{3,1,0,2:T(4,128)(2,1)S(1)}, u32[]{:S(2)}, u32[]{:S(2)}) async-start(bf16[1,3,16,256]{3,1,0,2:T(4,128)(2,1)} %copy.251), calls=%async_computation.8 | async-start | bytes 65536 | tf_op jit(solution)/shard_map/all_to_all | solution.py:199
Sparse Core Ops, SparseCore 0:
  97.9 11.4 reduce-scatter.3
where the time goes:
time: 143 us; the launch traced here: 142 us
  waiting for transfers between devices  55.6 us (39%)
  starting transfers between devices  44.9 us (31%)
  local copies, waits for them, and re-layouts  15.2 us (11%)
  between operations  14.6 us (10%)
  blocking collectives  4.76 us (3%)
  other arithmetic  3.89 us (3%)
  matrix products  3.38 us (2%)
    all_to_all x1, starting transfers between devices, body(): lax.all_to_all(to_columns(attn_values), 'band', split_axis=0, concat_axis...  7.39 us
    all_to_all x1, waiting for transfers between devices, body(): lax.all_to_all(far_out, 'band', split_axis=2, concat_axis=0, tiled=True)  6.62 us
    all_to_all x1, waiting for transfers between devices, body(): lax.all_to_all(to_columns(queries), 'band', split_axis=0, concat_axis=2,...  6.45 us
    all_to_all x1, waiting for transfers between devices, body(): lax.all_to_all(to_columns(log_all), 'band', split_axis=0, concat_axis=2,...  6.39 us
    all_to_all x1, starting transfers between devices, body(): lax.all_to_all(to_columns(attn_keys), 'band', split_axis=0, concat_axis=2...  6.01 us
    all_to_all x1, waiting for transfers between devices, body(): lax.all_to_all(grad_k[:, 3:].astype(jnp.bfloat16), 'band', split_axis=2,...  5.98 us
    all_to_all x1, waiting for transfers between devices, body(): lax.all_to_all(grad_q[:, 3:].astype(jnp.bfloat16), 'band', split_axis=2,...  5.98 us
    unnamed x23, local copies, waits for them, and re-layouts  5.5 us
  transfers between devices with their start and end apart: 12, of which 10 were waited for; matrix products, arithmetic and copies ran while one was open for 11% of the time, Pallas kernels for 0%

commit v1 on v0

v1 whole, which is shorter than its diff:
```python
import functools

import jax
import jax.numpy as jnp
from jax import lax
from jax.experimental import pallas as pl
from jax.experimental.pallas import tpu as pltpu
from jax.sharding import PartitionSpec as P

HEAD_DIM = 64
CHUNK = 16
MESH = pl.DeviceIdType.MESH
F32 = jnp.float32
BF16 = jnp.bfloat16
I32 = jnp.int32


def dot(a, b):
    return jnp.dot(a, b, preferred_element_type=F32)


def dot_bt(a, b):
    return lax.dot_general(a, b, (((1,), (1,)), ((), ())), preferred_element_type=F32)


def dot_at(a, b):
    return lax.dot_general(a, b, (((0,), (0,)), ((), ())), preferred_element_type=F32)


def iota(shape, axis):
    return lax.broadcasted_iota(I32, shape, axis)


def split3(x):
    high = x.astype(BF16)
    rest = x - high.astype(F32)
    mid = rest.astype(BF16)
    low = (rest - mid.astype(F32)).astype(BF16)
    return high, mid, low


def kernel(
    n, groups,
    q_ref, k_ref, v_ref, w_ref, go_ref, ax_ref,
    layer_ref, dq_ref, dk_ref, dv_ref,
    s1, r1, s2, r2, s3, r3, s4, r4, go_in, part_out, part_in,
    send_sem, recv_sem, head_send, head_recv,
):
    me = lax.axis_index("band")
    mine = lax.axis_index("head")
    _, planes, R, F = q_ref.shape
    rows = planes * R
    half = F // 2
    heads = F // HEAD_DIM
    width = w_ref.shape[1]
    RH = R // groups

    barrier = pltpu.get_barrier_semaphore()

    @pl.loop(1, n)
    def _(d):
        peer = lax.rem(me + d, n)
        pl.semaphore_signal(barrier, inc=1, device_id={"band": peer}, device_id_type=MESH)

    for d in range(1, groups):
        peer = lax.rem(mine + d, groups)
        pl.semaphore_signal(barrier, inc=1, device_id={"head": peer}, device_id_type=MESH)

    channels = 4 * planes

    def pack_matrix():
        r = iota((R * CHUNK, channels * R), 0)
        s = iota((R * CHUNK, channels * R), 1)
        return jnp.where(s == (r & (CHUNK - 1)) * R + (r // CHUNK), 1.0, 0.0).astype(BF16)

    def unpack_matrix():
        s = iota((channels * R, R * CHUNK), 0)
        r = iota((channels * R, R * CHUNK), 1)
        return jnp.where(s == (r & (CHUNK - 1)) * R + (r // CHUNK), 1.0, 0.0).astype(BF16)

    pack = pack_matrix()
    unpack = unpack_matrix()

    def wide(parts):
        parts = list(parts)
        return jnp.concatenate(parts + [jnp.zeros((rows, F), BF16)], axis=0)

    def narrow(a, b):
        return jnp.concatenate([a[:, :half], a[:, half:], b[:, :half], b[:, half:]], axis=0)

    def exchange_start(phase, src, dst, x):
        src[...] = dot(pack, x).astype(BF16)
        own = pl.ds(pl.multiple_of(me * CHUNK, CHUNK), CHUNK)

        @pl.loop(1, n)
        def _(d):
            copy_of(phase, src, dst, d).start()

        dst[own, :] = src[own, :]

    def copy_of(phase, src, dst, d):
        peer = lax.rem(me + d, n)
        return pltpu.make_async_remote_copy(
            src_ref=src.at[pl.ds(pl.multiple_of(peer * CHUNK, CHUNK), CHUNK)],
            dst_ref=dst.at[pl.ds(pl.multiple_of(me * CHUNK, CHUNK), CHUNK)],
            send_sem=send_sem.at[phase, d],
            recv_sem=recv_sem.at[phase, d],
            device_id={"band": peer},
            device_id_type=MESH,
        )

    def exchange_wait(phase, src, dst):
        @pl.loop(1, n)
        def _(d):
            copy_of(phase, src, dst, d).wait_recv()

        return dst[...]

    def exchange_end(phase, src, dst):
        @pl.loop(1, n)
        def _(d):
            copy_of(phase, src, dst, d).wait_send()

    def unwide(y):
        x = dot(unpack[: 3 * rows], y)
        return x[:rows], x[rows : 2 * rows], x[2 * rows :]

    def unnarrow(y):
        x = dot(unpack, y)
        a = jnp.concatenate([x[:rows], x[rows : 2 * rows]], axis=1)
        b = jnp.concatenate([x[2 * rows : 3 * rows], x[3 * rows :]], axis=1)
        return a, b

    q_row = q_ref[0].reshape(rows, F)
    k_row = k_ref[0].reshape(rows, F)
    v_row = v_ref[0].reshape(rows, F)

    def place(s):
        to = jnp.zeros_like(s)
        for w in range(groups):
            owner = lax.rem(mine - w + groups, groups)
            for p in range(planes):
                first = (w * planes + p) * RH
                inside = (s >= first) & (s < first + RH)
                to = jnp.where(inside, s - first + p * R + owner * RH, to)
        return to

    gather_rows = jnp.where(
        iota((rows, rows), 0) == place(iota((rows, rows), 1)), 1.0, 0.0
    ).astype(BF16)
    spread_rows = jnp.where(
        iota((rows, rows), 1) == place(iota((rows, rows), 0)), 1.0, 0.0
    ).astype(BF16)

    lane = iota((1, F), 1)
    lane_head = lane // HEAD_DIM
    lane_in = lane & (HEAD_DIM - 1)
    head_masks = [jnp.where(lane_head == h, 1.0, 0.0).astype(BF16) for h in range(heads)]

    def stack(x):
        return jnp.concatenate([x * head_masks[h] for h in range(heads)], axis=0)

    def fold(y):
        out = y[:rows]
        for h in range(1, heads):
            out = jnp.where(lane_head == h, y[h * rows : (h + 1) * rows], out)
        return out

    e_in, e_out = iota((F, F), 0), iota((F, F), 1)
    same_head = (e_in // HEAD_DIM) == (e_out // HEAD_DIM)
    place_in = e_in & (HEAD_DIM - 1)
    sum_all = jnp.where(same_head, 1.0, 0.0).astype(BF16)
    sum_first = jnp.where(same_head & (place_in < 3), 1.0, 0.0).astype(BF16)
    sum_second = jnp.where(same_head & (place_in >= 3) & (place_in < 6), 1.0, 0.0).astype(BF16)

    def columns(x):
        return jnp.concatenate(
            [x[:, h * HEAD_DIM : h * HEAD_DIM + 1] for h in range(heads)], axis=0
        )

    axis_of = [ax_ref[p, 0] for p in range(planes)] + [ax_ref[p, 1] for p in range(planes)]
    partner = []
    for b in range(2 * planes):
        found = jnp.int32(0)
        for c in range(2 * planes):
            if c != b:
                found = found + jnp.where(axis_of[b] == axis_of[c], jnp.int32(c), jnp.int32(0))
        partner.append(found)

    def bias_of(side):
        row, col = iota((rows, 2 * rows), 0), iota((rows, 2 * rows), 1)
        key_block = jnp.zeros_like(col)
        for b in range(1, 2 * planes):
            key_block = key_block + jnp.where(col >= b * R, 1, 0)
        block = jnp.zeros_like(row)
        for b in range(1, planes):
            block = block + jnp.where(row >= b * R, 1, 0)
        wanted = jnp.zeros_like(row)
        for b in range(planes):
            wanted = jnp.where(block == b, partner[side * planes + b], wanted)
        allowed = key_block == wanted
        if side == 0:
            allowed = allowed | (key_block == block)
        bias = jnp.where(allowed, 0.0, -1e30)
        return jnp.concatenate([bias] * heads, axis=0)

    bias_row, bias_col = bias_of(0), bias_of(1)
    scale = HEAD_DIM**-0.5

    pl.semaphore_wait(barrier, n - 1 + groups - 1)

    head_copies = []
    for d in range(1, groups):
        copy = pltpu.make_async_remote_copy(
            src_ref=go_ref.at[0],
            dst_ref=go_in.at[d - 1],
            send_sem=head_send.at[0, d],
            recv_sem=head_recv.at[0, d],
            device_id={"head": lax.rem(mine + d, groups)},
            device_id_type=MESH,
        )
        copy.start()
        head_copies.append(copy)
    exchange_start(0, s1, r1, wide([q_row, k_row, v_row]))

    for copy in head_copies:
        copy.wait_recv()
    pieces = [go_ref[0].astype(F32).reshape(planes * RH, width)]
    for d in range(1, groups):
        pieces.append(go_in[d - 1].astype(F32).reshape(planes * RH, width))
    grad_rows = jnp.concatenate(pieces, axis=0).astype(BF16)
    g_raw = dot_bt(grad_rows, w_ref[...]).astype(BF16)
    g_row = dot(gather_rows, g_raw).astype(BF16)

    q_stack_row, g_stack_row = stack(q_row), stack(g_row)

    q_col, k_col, v_col = (x.astype(BF16) for x in unwide(exchange_wait(0, s1, r1)))
    keys = jnp.concatenate([k_row, k_col], axis=0)
    values = jnp.concatenate([v_row, v_col], axis=0)

    def forward(q_stack, bias):
        scores = dot_bt(q_stack, keys) * scale + bias
        top = jnp.max(scores, axis=1, keepdims=True)
        e = jnp.exp(scores - top)
        total = jnp.sum(e, axis=1, keepdims=True)
        prob = (e * (1.0 / total)).astype(BF16)
        out = fold(dot(prob, values))
        log_sum = top + jnp.log(total)
        spread = fold(jnp.broadcast_to(log_sum, (heads * rows, F)))
        return scores, out, spread

    q_stack_col = stack(q_col)
    scores_col, far_out, far_total = forward(q_stack_col, bias_col)
    high, mid, low = split3(far_total)
    zero = jnp.zeros_like(far_total)
    stat = jnp.where(
        lane_in == 0,
        high.astype(F32),
        jnp.where(lane_in == 1, mid.astype(F32), jnp.where(lane_in == 2, low.astype(F32), zero)),
    ).astype(BF16)
    exchange_start(1, s2, r2, narrow(far_out.astype(BF16), stat))

    scores_row, near_out, near_total = forward(q_stack_row, bias_row)

    far_out, far_stat = unnarrow(exchange_wait(1, s2, r2))
    far_total = dot(far_stat.astype(BF16), sum_first)
    top = jnp.maximum(near_total, far_total)
    log_all = top + jnp.log(jnp.exp(near_total - top) + jnp.exp(far_total - top))
    attended = (
        near_out * jnp.exp(near_total - log_all) + far_out * jnp.exp(far_total - log_all)
    ).astype(BF16)
    product = g_row.astype(F32) * attended.astype(F32)
    sums = dot(jnp.concatenate(split3(product), axis=0), sum_all)
    delta = sums[:rows] + sums[rows : 2 * rows] + sums[2 * rows :]

    stat = zero
    for place_at, piece in enumerate(split3(log_all) + split3(delta)):
        stat = jnp.where(lane_in == place_at, piece.astype(F32), stat)
    exchange_start(2, s3, r3, narrow(g_row, stat.astype(BF16)))

    part = dot(dot(spread_rows, attended).astype(BF16), w_ref[...])
    part_rows = planes * RH
    layer_copies = []
    for d in range(1, groups):
        piece = part[d * part_rows : (d + 1) * part_rows]
        part_out[d - 1] = piece.reshape(planes, RH, width).astype(BF16)
        copy = pltpu.make_async_remote_copy(
            src_ref=part_out.at[d - 1],
            dst_ref=part_in.at[d - 1],
            send_sem=head_send.at[1, d],
            recv_sem=head_recv.at[1, d],
            device_id={"head": lax.rem(mine - d + groups, groups)},
            device_id_type=MESH,
        )
        copy.start()
        layer_copies.append(copy)

    def backward(scores, q_stack, g_stack, log_spread, delta_spread):
        prob = jnp.exp(scores - columns(log_spread)).astype(BF16)
        grad = dot_bt(g_stack, values)
        step = (prob.astype(F32) * (grad - columns(delta_spread)) * scale).astype(BF16)
        return fold(dot(step, keys)), dot_at(step, q_stack), dot_at(prob, g_stack)

    dq_row, dk_part, dv_part = backward(scores_row, q_stack_row, g_stack_row, log_all, delta)

    g_col, col_stat = unnarrow(exchange_wait(2, s3, r3))
    col_stat = col_stat.astype(BF16)
    log_col, delta_col = dot(col_stat, sum_first), dot(col_stat, sum_second)
    dq_col, dk_more, dv_more = backward(
        scores_col, q_stack_col, stack(g_col.astype(BF16)), log_col, delta_col
    )
    dk_all, dv_all = dk_part + dk_more, dv_part + dv_more
    exchange_start(
        3, s4, r4, wide([dq_col.astype(BF16), dk_all[rows:].astype(BF16), dv_all[rows:].astype(BF16)])
    )

    total = part[:part_rows]
    for d in range(1, groups):
        layer_copies[d - 1].wait_recv()
        total = total + part_in[d - 1].astype(F32).reshape(part_rows, width)
    layer_ref[0] = total.reshape(planes, RH, width).astype(BF16)
    for copy in head_copies + layer_copies:
        copy.wait_send()
    exchange_end(0, s1, r1)
    exchange_end(1, s2, r2)
    exchange_end(2, s3, r3)

    back_q, back_k, back_v = unwide(exchange_wait(3, s4, r4))
    dq_ref[0] = (dq_row + back_q).astype(BF16).reshape(planes, R, F)
    dk_ref[0] = (dk_all[:rows] + back_k).astype(BF16).reshape(planes, R, F)
    dv_ref[0] = (dv_all[:rows] + back_v).astype(BF16).reshape(planes, R, F)
    exchange_end(3, s4, r4)


def solution(mesh):
    n, groups = mesh.shape["band"], mesh.shape["head"]

    def body(queries, attn_keys, attn_values, out_proj, grad_out, plane_axes):
        _, planes, R, F = queries.shape
        width = out_proj.shape[1]
        vmem = pl.BlockSpec(memory_space=pltpu.VMEM)
        smem = pl.BlockSpec(memory_space=pltpu.SMEM)
        wide = pltpu.VMEM((R * CHUNK, F), BF16)
        narrow = pltpu.VMEM((R * CHUNK, F // 2), BF16)
        part = pltpu.VMEM((groups - 1, planes, R // groups, width), BF16)
        like = jax.ShapeDtypeStruct(queries.shape, BF16)
        return pl.pallas_call(
            functools.partial(kernel, n, groups),
            out_shape=(jax.ShapeDtypeStruct(grad_out.shape, BF16), like, like, like),
            in_specs=[vmem] * 5 + [smem],
            out_specs=(vmem,) * 4,
            scratch_shapes=[
                wide, wide, narrow, narrow, narrow, narrow, wide, wide, part, part, part,
                pltpu.SemaphoreType.DMA((4, n)),
                pltpu.SemaphoreType.DMA((4, n)),
                pltpu.SemaphoreType.DMA((2, groups)),
                pltpu.SemaphoreType.DMA((2, groups)),
            ],
            compiler_params=pltpu.CompilerParams(
                collective_id=0, has_side_effects=True, vmem_limit_bytes=60 * 1024 * 1024
            ),
        )(queries, attn_keys, attn_values, out_proj, grad_out, plane_axes)

    rows = P("band", None, None, "head")
    cols = P("band", None, "head", None)
    return jax.shard_map(
        body,
        mesh=mesh,
        in_specs=(rows, rows, rows, P("head", None), cols, P()),
        out_specs=(cols, rows, rows, rows),
        check_vma=False,
    )
```

time: 143 us -> 35.8 us (0.25)
  waiting for transfers between devices: 55.6 us -> 0 us
  starting transfers between devices: 44.9 us -> 0 us
  Pallas kernels: 0 us -> 29.9 us
  between operations: 14.6 us -> 0.65 us
  local copies, waits for them, and re-layouts: 15.2 us -> 4.87 us
  blocking collectives: 4.76 us -> 0 us
  other arithmetic: 3.89 us -> 0 us
  matrix products: 3.38 us -> 0 us
    all_to_all x11 -> x0, waiting for transfers between devices: 55.6 us -> none  [the longest x1 6.62 us: body(): lax.all_to_all(far_out, 'band', split_axis=2, concat_axis=0, tiled=True)]
    all_to_all x11 -> x0, starting transfers between devices: 44.8 us -> none  [the longest x1 7.39 us: body(): lax.all_to_all(to_columns(attn_values), 'band', split_axis=0, concat_axis...]
    pallas_call x0 -> x1, Pallas kernels: none -> 29.9 us  [body(): pl.pallas_call(functools.partial(kernel, n, groups), out_shape=(jax.Shape...]
    all_gather x1 -> x0, blocking collectives: 4.76 us -> none  [body(): lax.all_gather(grad_out, 'head', axis=2, tiled=True)]
    dot_general x15 -> x0, matrix products: 3.38 us -> none  [the longest x1 0.38 us: backward_core(): jnp.einsum('bhac,bahe->bche', cross_prob, grad_heads, preferred_element_t...]
    gather x4 -> x0, local copies, waits for them, and re-layouts: 2.26 us -> none  [the longest x1 0.57 us: backward_core(): grad_value = jnp.take(toward_values, partner, axis=0)]
    slice x13 -> x0, local copies, waits for them, and re-layouts: 2.22 us -> none  [the longest x2 0.64 us: body(): grad_v[:, 3:].astype(jnp.bfloat16)]
    broadcast_in_dim x6 -> x0, local copies, waits for them, and re-layouts: 1.99 us -> none  [the longest x3 1.49 us: body(): near_total, near_out, far_total, far_out = lax.map(forward_fresh, lines)]
  transfers between devices with their start and end apart: 12 -> 0, of which waited for: 10 -> 0; matrix products, arithmetic and copies ran while one was open for 11% -> 0% of each run, Pallas kernels for 0% -> 0%
where the time goes in v1:
time: 35.8 us; the launch traced here: 35.4 us
  Pallas kernels  29.9 us (84%)
  local copies, waits for them, and re-layouts  4.87 us (14%)
  between operations  0.65 us (2%)
    pallas_call x1, Pallas kernels, body(): pl.pallas_call(functools.partial(kernel, n, groups), out_shape=(jax.Shape...  29.9 us
    unnamed x11, local copies, waits for them, and re-layouts  4.87 us

profile of v1, /device:TPU:0, one launch (start us, length us, event | category | flops | bytes accessed | tf_op | source)
XLA Modules:
  0.0 35.4 jit_solution(17784936548605881667)
XLA Ops:
  0.6 1.3 %copy.10.ax_ref = s32[3,2]{1,0:T(4,128)} copy(s32[3,2]{0,1:T(2,128)} %param.11) | data formatting | bytes 48 | tf_op args[5]
  2.0 29.9 %shard_map.93 = (bf16[1,3,8,1024]{3,2,1,0:T(8,128)(2,1)}, bf16[1,3,16,256]{3,2,1,0:T(8,128)(2,1)}, bf16[1,3,16,256]{3,2,1,0:T(8,128)(2,1)}, bf16[1,3,16,256]{3,2,1,0:T(8,128)(2,1)}) custom-call(bf16[1,3,16,256]{3,2,1,0:T(8,128)(2,1)} %q_ref.1, bf16[1,3,16,256]{3,2,1,0:T(8,128)(2,1)} %k_ref.1, bf16[1,3,16,256]{3,2,1,0:T(8,128)(2,1)} %v_ref.1, ...), custom_call_target="tpu_custom_call" | custom-call | tf_op jit(solution)/shard_map/pallas_call | solution.py:347
  31.9 0.0 copy-start.2
  31.9 1.4 %copy.15 = bf16[1,3,8,1024]{3,2,1,0:T(8,128)(2,1)} copy(bf16[1,3,8,1024]{3,2,1,0:T(8,128)(2,1)} %get-tuple-element.8) | data formatting | bytes 98304
  33.3 0.0 copy-done.2
  33.3 0.0 copy-start.1
  33.3 0.6 %copy.16 = bf16[1,3,16,256]{3,2,1,0:T(8,128)(2,1)} copy(bf16[1,3,16,256]{3,2,1,0:T(8,128)(2,1)S(1)} %copy-done.2) | data formatting | bytes 49152
  33.9 0.1 copy-done.1
  34.1 0.0 copy-start
  34.1 0.6 %copy.17 = bf16[1,3,16,256]{3,2,1,0:T(8,128)(2,1)} copy(bf16[1,3,16,256]{3,2,1,0:T(8,128)(2,1)S(1)} %copy-done.1) | data formatting | bytes 49152
  34.7 0.1 copy-done
  34.8 0.6 %copy.18 = bf16[1,3,16,256]{3,2,1,0:T(8,128)(2,1)} copy(bf16[1,3,16,256]{3,2,1,0:T(8,128)(2,1)S(1)} %copy-done) | data formatting | bytes 49152
Async XLA Ops:
  31.9 1.4 %copy-start.2 = (bf16[1,3,16,256]{3,2,1,0:T(8,128)(2,1)S(1)}, bf16[1,3,16,256]{3,2,1,0:T(8,128)(2,1)}, u32[]{:S(2)}) copy-start(bf16[1,3,16,256]{3,2,1,0:T(8,128)(2,1)} %get-tuple-element.9) | copy-start | bytes 73732
  33.3 0.7 %copy-start.1 = (bf16[1,3,16,256]{3,2,1,0:T(8,128)(2,1)S(1)}, bf16[1,3,16,256]{3,2,1,0:T(8,128)(2,1)}, u32[]{:S(2)}) copy-start(bf16[1,3,16,256]{3,2,1,0:T(8,128)(2,1)} %get-tuple-element.10) | copy-start | bytes 73732
  34.1 0.7 %copy-start = (bf16[1,3,16,256]{3,2,1,0:T(8,128)(2,1)S(1)}, bf16[1,3,16,256]{3,2,1,0:T(8,128)(2,1)}, u32[]{:S(2)}) copy-start(bf16[1,3,16,256]{3,2,1,0:T(8,128)(2,1)} %get-tuple-element.11) | copy-start | bytes 73732

commit v2 on v1

--- a/solution.py
+++ b/solution.py
@@ -41,10 +41,11 @@
 
 def kernel(
     n, groups,
+    q_hbm, k_hbm, v_hbm, w_hbm, go_hbm, ax_hbm,
+    layer_ref, dq_ref, dk_ref, dv_ref,
     q_ref, k_ref, v_ref, w_ref, go_ref, ax_ref,
-    layer_ref, dq_ref, dk_ref, dv_ref,
     s1, r1, s2, r2, s3, r3, s4, r4, go_in, part_out, part_in,
-    send_sem, recv_sem, head_send, head_recv,
+    send_sem, recv_sem, head_send, head_recv, load_sem,
 ):
     me = lax.axis_index("band")
     mine = lax.axis_index("head")
@@ -66,6 +67,18 @@
         peer = lax.rem(mine + d, groups)
         pl.semaphore_signal(barrier, inc=1, device_id={"head": peer}, device_id_type=MESH)
 
+    loads = [
+        pltpu.make_async_copy(src, dst, load_sem.at[at])
+        for at, (src, dst) in enumerate(
+            [
+                (q_hbm, q_ref), (k_hbm, k_ref), (v_hbm, v_ref),
+                (ax_hbm, ax_ref), (go_hbm, go_ref), (w_hbm, w_ref),
+            ]
+        )
+    ]
+    for load in loads:
+        load.start()
+
     channels = 4 * planes
 
     def pack_matrix():
@@ -89,37 +102,43 @@
         return jnp.concatenate([a[:, :half], a[:, half:], b[:, :half], b[:, half:]], axis=0)
 
     def exchange_start(phase, src, dst, x):
-        src[...] = dot(pack, x).astype(BF16)
+        if x is not None:
+            src[...] = dot(pack, x).astype(BF16)
         own = pl.ds(pl.multiple_of(me * CHUNK, CHUNK), CHUNK)
 
-        @pl.loop(1, n)
-        def _(d):
-            copy_of(phase, src, dst, d).start()
+        @pl.loop(0, n - 1)
+        def _(i):
+            away = (i + 1) // 2
+            d = n // 2 + away * (1 - 2 * lax.rem(i, 2))
+            peer = lax.rem(me + d, n)
+            pltpu.make_async_remote_copy(
+                src_ref=src.at[pl.ds(pl.multiple_of(peer * CHUNK, CHUNK), CHUNK)],
+                dst_ref=dst.at[own],
+                send_sem=send_sem.at[phase],
+                recv_sem=recv_sem.at[phase],
+                device_id={"band": peer},
+                device_id_type=MESH,
+            ).start()
 
         dst[own, :] = src[own, :]
 
-    def copy_of(phase, src, dst, d):
-        peer = lax.rem(me + d, n)
+    def all_copies(phase, src, dst):
+        others = pl.ds(0, (n - 1) * CHUNK)
         return pltpu.make_async_remote_copy(
-            src_ref=src.at[pl.ds(pl.multiple_of(peer * CHUNK, CHUNK), CHUNK)],
-            dst_ref=dst.at[pl.ds(pl.multiple_of(me * CHUNK, CHUNK), CHUNK)],
-            send_sem=send_sem.at[phase, d],
-            recv_sem=recv_sem.at[phase, d],
-            device_id={"band": peer},
+            src_ref=src.at[others],
+            dst_ref=dst.at[others],
+            send_sem=send_sem.at[phase],
+            recv_sem=recv_sem.at[phase],
+            device_id={"band": lax.rem(me + 1, n)},
             device_id_type=MESH,
         )
 
     def exchange_wait(phase, src, dst):
-        @pl.loop(1, n)
-        def _(d):
-            copy_of(phase, src, dst, d).wait_recv()
-
+        all_copies(phase, src, dst).wait_recv()
         return dst[...]
 
     def exchange_end(phase, src, dst):
-        @pl.loop(1, n)
-        def _(d):
-            copy_of(phase, src, dst, d).wait_send()
+        all_copies(phase, src, dst).wait_send()
 
     def unwide(y):
         x = dot(unpack[: 3 * rows], y)
@@ -131,9 +150,6 @@
         b = jnp.concatenate([x[2 * rows : 3 * rows], x[3 * rows :]], axis=1)
         return a, b
 
-    q_row = q_ref[0].reshape(rows, F)
-    k_row = k_ref[0].reshape(rows, F)
-    v_row = v_ref[0].reshape(rows, F)
 
     def place(s):
         to = jnp.zeros_like(s)
@@ -178,7 +194,9 @@
             [x[:, h * HEAD_DIM : h * HEAD_DIM + 1] for h in range(heads)], axis=0
         )
 
-    axis_of = [ax_ref[p, 0] for p in range(planes)] + [ax_ref[p, 1] for p in range(planes)]
+    for load in loads[:4]:
+        load.wait()
+    axis_of = [ax_ref[0, p] for p in range(planes)] + [ax_ref[1, p] for p in range(planes)]
     partner = []
     for b in range(2 * planes):
         found = jnp.int32(0)
@@ -207,22 +225,30 @@
     bias_row, bias_col = bias_of(0), bias_of(1)
     scale = HEAD_DIM**-0.5
 
+    q_row = q_ref[0].reshape(rows, F)
+    k_row = k_ref[0].reshape(rows, F)
+    v_row = v_ref[0].reshape(rows, F)
+    s1[...] = dot(pack, wide([q_row, k_row, v_row])).astype(BF16)
+    q_stack_row = stack(q_row)
+
     pl.semaphore_wait(barrier, n - 1 + groups - 1)
 
     head_copies = []
     for d in range(1, groups):
         copy = pltpu.make_async_remote_copy(
-            src_ref=go_ref.at[0],
+            src_ref=go_hbm.at[0],
             dst_ref=go_in.at[d - 1],
-            send_sem=head_send.at[0, d],
-            recv_sem=head_recv.at[0, d],
+            send_sem=head_send.at[0, d - 1],
+            recv_sem=head_recv.at[0, d - 1],
             device_id={"head": lax.rem(mine + d, groups)},
             device_id_type=MESH,
         )
         copy.start()
         head_copies.append(copy)
-    exchange_start(0, s1, r1, wide([q_row, k_row, v_row]))
-
+    exchange_start(0, s1, r1, None)
+
+    for load in loads[4:]:
+        load.wait()
     for copy in head_copies:
         copy.wait_recv()
     pieces = [go_ref[0].astype(F32).reshape(planes * RH, width)]
@@ -232,7 +258,7 @@
     g_raw = dot_bt(grad_rows, w_ref[...]).astype(BF16)
     g_row = dot(gather_rows, g_raw).astype(BF16)
 
-    q_stack_row, g_stack_row = stack(q_row), stack(g_row)
+    g_stack_row = stack(g_row)
 
     q_col, k_col, v_col = (x.astype(BF16) for x in unwide(exchange_wait(0, s1, r1)))
     keys = jnp.concatenate([k_row, k_col], axis=0)
@@ -261,6 +287,7 @@
     exchange_start(1, s2, r2, narrow(far_out.astype(BF16), stat))
 
     scores_row, near_out, near_total = forward(q_stack_row, bias_row)
+    product_row = dot_bt(g_stack_row, values)
 
     far_out, far_stat = unnarrow(exchange_wait(1, s2, r2))
     far_total = dot(far_stat.astype(BF16), sum_first)
@@ -287,27 +314,29 @@
         copy = pltpu.make_async_remote_copy(
             src_ref=part_out.at[d - 1],
             dst_ref=part_in.at[d - 1],
-            send_sem=head_send.at[1, d],
-            recv_sem=head_recv.at[1, d],
+            send_sem=head_send.at[1, d - 1],
+            recv_sem=head_recv.at[1, d - 1],
             device_id={"head": lax.rem(mine - d + groups, groups)},
             device_id_type=MESH,
         )
         copy.start()
         layer_copies.append(copy)
 
-    def backward(scores, q_stack, g_stack, log_spread, delta_spread):
+    def backward(scores, q_stack, g_stack, grad, log_spread, delta_spread):
         prob = jnp.exp(scores - columns(log_spread)).astype(BF16)
-        grad = dot_bt(g_stack, values)
         step = (prob.astype(F32) * (grad - columns(delta_spread)) * scale).astype(BF16)
         return fold(dot(step, keys)), dot_at(step, q_stack), dot_at(prob, g_stack)
 
-    dq_row, dk_part, dv_part = backward(scores_row, q_stack_row, g_stack_row, log_all, delta)
+    dq_row, dk_part, dv_part = backward(
+        scores_row, q_stack_row, g_stack_row, product_row, log_all, delta
+    )
 
     g_col, col_stat = unnarrow(exchange_wait(2, s3, r3))
     col_stat = col_stat.astype(BF16)
     log_col, delta_col = dot(col_stat, sum_first), dot(col_stat, sum_second)
+    g_stack_col = stack(g_col.astype(BF16))
     dq_col, dk_more, dv_more = backward(
-        scores_col, q_stack_col, stack(g_col.astype(BF16)), log_col, delta_col
+        scores_col, q_stack_col, g_stack_col, dot_bt(g_stack_col, values), log_col, delta_col
     )
     dk_all, dv_all = dk_part + dk_more, dv_part + dv_more
     exchange_start(
@@ -332,34 +361,60 @@
     exchange_end(3, s4, r4)
 
 
+def store_kernel(*refs):
+    sources, targets, sem = refs[:4], refs[4:8], refs[8]
+    copies = [
+        pltpu.make_async_copy(src, dst, sem.at[at])
+        for at, (src, dst) in enumerate(zip(sources, targets))
+    ]
+    for copy in copies:
+        copy.start()
+    for copy in copies:
+        copy.wait()
+
+
 def solution(mesh):
     n, groups = mesh.shape["band"], mesh.shape["head"]
 
     def body(queries, attn_keys, attn_values, out_proj, grad_out, plane_axes):
         _, planes, R, F = queries.shape
         width = out_proj.shape[1]
+        whole = pl.BlockSpec(memory_space=pl.ANY)
         vmem = pl.BlockSpec(memory_space=pltpu.VMEM)
-        smem = pl.BlockSpec(memory_space=pltpu.SMEM)
         wide = pltpu.VMEM((R * CHUNK, F), BF16)
         narrow = pltpu.VMEM((R * CHUNK, F // 2), BF16)
         part = pltpu.VMEM((groups - 1, planes, R // groups, width), BF16)
-        like = jax.ShapeDtypeStruct(queries.shape, BF16)
-        return pl.pallas_call(
+        shapes = [grad_out.shape] + [queries.shape] * 3
+        results = pl.pallas_call(
             functools.partial(kernel, n, groups),
-            out_shape=(jax.ShapeDtypeStruct(grad_out.shape, BF16), like, like, like),
-            in_specs=[vmem] * 5 + [smem],
+            out_shape=tuple(pltpu.VMEM(shape, BF16) for shape in shapes),
+            in_specs=[whole] * 6,
             out_specs=(vmem,) * 4,
             scratch_shapes=[
+                pltpu.VMEM(queries.shape, BF16),
+                pltpu.VMEM(queries.shape, BF16),
+                pltpu.VMEM(queries.shape, BF16),
+                pltpu.VMEM(out_proj.shape, BF16),
+                pltpu.VMEM(grad_out.shape, BF16),
+                pltpu.SMEM(plane_axes.shape[::-1], I32),
                 wide, wide, narrow, narrow, narrow, narrow, wide, wide, part, part, part,
-                pltpu.SemaphoreType.DMA((4, n)),
-                pltpu.SemaphoreType.DMA((4, n)),
-                pltpu.SemaphoreType.DMA((2, groups)),
-                pltpu.SemaphoreType.DMA((2, groups)),
+                pltpu.SemaphoreType.DMA((4,)),
+                pltpu.SemaphoreType.DMA((4,)),
+                pltpu.SemaphoreType.DMA((2, groups - 1)),
+                pltpu.SemaphoreType.DMA((2, groups - 1)),
+                pltpu.SemaphoreType.DMA((6,)),
             ],
             compiler_params=pltpu.CompilerParams(
-                collective_id=0, has_side_effects=True, vmem_limit_bytes=60 * 1024 * 1024
+                collective_id=0, has_side_effects=True, vmem_limit_bytes=56 * 1024 * 1024
             ),
-        )(queries, attn_keys, attn_values, out_proj, grad_out, plane_axes)
+        )(queries, attn_keys, attn_values, out_proj, grad_out, plane_axes.T)
+        return pl.pallas_call(
+            store_kernel,
+            out_shape=tuple(jax.ShapeDtypeStruct(shape, BF16) for shape in shapes),
+            in_specs=[vmem] * 4,
+            out_specs=(whole,) * 4,
+            scratch_shapes=[pltpu.SemaphoreType.DMA((4,))],
+        )(*[pltpu.with_memory_space_constraint(r, pltpu.VMEM) for r in results])
 
     rows = P("band", None, None, "head")
     cols = P("band", None, "head", None)

time: 35.8 us -> 29.9 us (0.84)
  local copies, waits for them, and re-layouts: 4.87 us -> 0 us
  Pallas kernels: 29.9 us -> 29.1 us
    unnamed x11 -> x0, local copies, waits for them, and re-layouts: 4.87 us -> none
    pallas_call x1 -> x2, Pallas kernels: 29.9 us -> 29.1 us  [the longest x1 28.5 us: body(): pl.pallas_call(functools.partial(kernel, n, groups), out_shape=tuple((plt...]
where the time goes in v2:
time: 29.9 us; the launch traced here: 29.8 us
  Pallas kernels  29.1 us (97%)
  between operations  0.64 us (2%)
    pallas_call x1, Pallas kernels, body(): pl.pallas_call(functools.partial(kernel, n, groups), out_shape=tuple((plt...  28.5 us
    pallas_call x1, Pallas kernels, body(): pl.pallas_call(store_kernel, out_shape=tuple((jax.ShapeDtypeStruct(shape,...  0.68 us

profile of v2, /device:TPU:0, one launch (start us, length us, event | category | flops | bytes accessed | tf_op | source)
XLA Modules:
  0.0 29.8 jit_solution(2595929152224895783)
XLA Ops:
  0.6 28.5 %shard_map.93 = (bf16[1,3,8,1024]{3,2,1,0:T(8,128)(2,1)S(1)}, bf16[1,3,16,256]{3,2,1,0:T(8,128)(2,1)S(1)}, bf16[1,3,16,256]{3,2,1,0:T(8,128)(2,1)S(1)}, bf16[1,3,16,256]{3,2,1,0:T(8,128)(2,1)S(1)}) custom-call(bf16[1,3,16,256]{3,2,1,0:T(8,128)(2,1)} %q_hbm.1, bf16[1,3,16,256]{3,2,1,0:T(8,128)(2,1)} %k_hbm.1, bf16[1,3,16,256]{3,2,1,0:T(8,128)(2,1)} %v_hbm.1, ...), custom_call_target="tpu_custom_call" | custom-call | tf_op jit(solution)/shard_map/pallas_call | solution.py:388
  29.1 0.7 %shard_map.94 = (bf16[1,3,8,1024]{3,2,1,0:T(8,128)(2,1)}, bf16[1,3,16,256]{3,2,1,0:T(8,128)(2,1)}, bf16[1,3,16,256]{3,2,1,0:T(8,128)(2,1)}, bf16[1,3,16,256]{3,2,1,0:T(8,128)(2,1)}) custom-call(bf16[1,3,8,1024]{3,2,1,0:T(8,128)(2,1)S(1)} %get-tuple-element.8.refs_0_, bf16[1,3,16,256]{3,2,1,0:T(8,128)(2,1)S(1)} %get-tuple-element.9.refs_1_, ...), custom_call_target="tpu_custom_call" | custom-call | tf_op jit(solution)/shard_map/pallas_call | solution.py:411

commit v3 on v2

--- a/solution.py
+++ b/solution.py
@@ -188,6 +188,7 @@
     sum_all = jnp.where(same_head, 1.0, 0.0).astype(BF16)
     sum_first = jnp.where(same_head & (place_in < 3), 1.0, 0.0).astype(BF16)
     sum_second = jnp.where(same_head & (place_in >= 3) & (place_in < 6), 1.0, 0.0).astype(BF16)
+    sum_third = jnp.where(same_head & (place_in >= 6) & (place_in < 9), 1.0, 0.0).astype(BF16)
 
     def columns(x):
         return jnp.concatenate(
@@ -258,6 +259,7 @@
     g_raw = dot_bt(grad_rows, w_ref[...]).astype(BF16)
     g_row = dot(gather_rows, g_raw).astype(BF16)
 
+    exchange_start(1, s2, r2, narrow(g_row, jnp.zeros_like(g_row)))
     g_stack_row = stack(g_row)
 
     q_col, k_col, v_col = (x.astype(BF16) for x in unwide(exchange_wait(0, s1, r1)))
@@ -277,33 +279,58 @@
 
     q_stack_col = stack(q_col)
     scores_col, far_out, far_total = forward(q_stack_col, bias_col)
-    high, mid, low = split3(far_total)
-    zero = jnp.zeros_like(far_total)
-    stat = jnp.where(
-        lane_in == 0,
-        high.astype(F32),
-        jnp.where(lane_in == 1, mid.astype(F32), jnp.where(lane_in == 2, low.astype(F32), zero)),
-    ).astype(BF16)
-    exchange_start(1, s2, r2, narrow(far_out.astype(BF16), stat))
-
     scores_row, near_out, near_total = forward(q_stack_row, bias_row)
+    far_out = far_out.astype(BF16)
+
+    def head_sums(product):
+        sums = dot(jnp.concatenate(split3(product), axis=0), sum_all)
+        return sums[:rows] + sums[rows : 2 * rows] + sums[2 * rows :]
+
+    near_delta = head_sums(g_row.astype(F32) * near_out)
+    stat = jnp.zeros_like(far_total)
+    for at, piece in enumerate(split3(far_total) + split3(near_total) + split3(near_delta)):
+        stat = jnp.where(lane_in == at, piece.astype(F32), stat)
+    exchange_start(2, s3, r3, narrow(far_out, stat.astype(BF16)))
+
     product_row = dot_bt(g_stack_row, values)
-
-    far_out, far_stat = unnarrow(exchange_wait(1, s2, r2))
-    far_total = dot(far_stat.astype(BF16), sum_first)
-    top = jnp.maximum(near_total, far_total)
-    log_all = top + jnp.log(jnp.exp(near_total - top) + jnp.exp(far_total - top))
-    attended = (
-        near_out * jnp.exp(near_total - log_all) + far_out * jnp.exp(far_total - log_all)
-    ).astype(BF16)
-    product = g_row.astype(F32) * attended.astype(F32)
-    sums = dot(jnp.concatenate(split3(product), axis=0), sum_all)
-    delta = sums[:rows] + sums[rows : 2 * rows] + sums[2 * rows :]
-
-    stat = zero
-    for place_at, piece in enumerate(split3(log_all) + split3(delta)):
-        stat = jnp.where(lane_in == place_at, piece.astype(F32), stat)
-    exchange_start(2, s3, r3, narrow(g_row, stat.astype(BF16)))
+    g_col = unnarrow(exchange_wait(1, s2, r2))[0].astype(BF16)
+    g_stack_col = stack(g_col)
+    product_col = dot_bt(g_stack_col, values)
+    own_delta = head_sums(g_col.astype(F32) * far_out.astype(F32))
+
+    def combine(near_total, near_delta, far_total, far_delta):
+        top = jnp.maximum(near_total, far_total)
+        log_all = top + jnp.log(jnp.exp(near_total - top) + jnp.exp(far_total - top))
+        near_weight, far_weight = jnp.exp(near_total - log_all), jnp.exp(far_total - log_all)
+        delta = near_weight * near_delta + far_weight * far_delta
+        return log_all, delta, near_weight, far_weight
+
+    row_far_out, stat = unnarrow(exchange_wait(2, s3, r3))
+    stat = stat.astype(BF16)
+    row_far_delta = head_sums(g_row.astype(F32) * row_far_out)
+    log_col, delta_col, _, _ = combine(
+        dot(stat, sum_second), dot(stat, sum_third), far_total, own_delta
+    )
+    log_row, delta_row, near_weight, far_weight = combine(
+        near_total, near_delta, dot(stat, sum_first), row_far_delta
+    )
+
+    def backward(scores, q_stack, g_stack, grad, log_spread, delta_spread):
+        prob = jnp.exp(scores - columns(log_spread)).astype(BF16)
+        step = (prob.astype(F32) * (grad - columns(delta_spread)) * scale).astype(BF16)
+        return fold(dot(step, keys)), dot_at(step, q_stack), dot_at(prob, g_stack)
+
+    dq_col, dk_more, dv_more = backward(
+        scores_col, q_stack_col, g_stack_col, product_col, log_col, delta_col
+    )
+    dq_row, dk_part, dv_part = backward(
+        scores_row, q_stack_row, g_stack_row, product_row, log_row, delta_row
+    )
+    dk_all, dv_all = dk_part + dk_more, dv_part + dv_more
+    exchange_start(
+        3, s4, r4, wide([dq_col.astype(BF16), dk_all[rows:].astype(BF16), dv_all[rows:].astype(BF16)])
+    )
+    attended = (near_out * near_weight + row_far_out * far_weight).astype(BF16)
 
     part = dot(dot(spread_rows, attended).astype(BF16), w_ref[...])
     part_rows = planes * RH
@@ -321,27 +348,6 @@
         )
         copy.start()
         layer_copies.append(copy)
-
-    def backward(scores, q_stack, g_stack, grad, log_spread, delta_spread):
-        prob = jnp.exp(scores - columns(log_spread)).astype(BF16)
-        step = (prob.astype(F32) * (grad - columns(delta_spread)) * scale).astype(BF16)
-        return fold(dot(step, keys)), dot_at(step, q_stack), dot_at(prob, g_stack)
-
-    dq_row, dk_part, dv_part = backward(
-        scores_row, q_stack_row, g_stack_row, product_row, log_all, delta
-    )
-
-    g_col, col_stat = unnarrow(exchange_wait(2, s3, r3))
-    col_stat = col_stat.astype(BF16)
-    log_col, delta_col = dot(col_stat, sum_first), dot(col_stat, sum_second)
-    g_stack_col = stack(g_col.astype(BF16))
-    dq_col, dk_more, dv_more = backward(
-        scores_col, q_stack_col, g_stack_col, dot_bt(g_stack_col, values), log_col, delta_col
-    )
-    dk_all, dv_all = dk_part + dk_more, dv_part + dv_more
-    exchange_start(
-        3, s4, r4, wide([dq_col.astype(BF16), dk_all[rows:].astype(BF16), dv_all[rows:].astype(BF16)])
-    )
 
     total = part[:part_rows]
     for d in range(1, groups):

time: 29.9 us -> 24.9 us (0.83)
  Pallas kernels: 29.1 us -> 24.1 us
    pallas_call x1, Pallas kernels: 28.5 us -> 23.4 us  [body(): pl.pallas_call(functools.partial(kernel, n, groups), out_shape=tuple((plt...]
where the time goes in v3:
time: 24.9 us; the launch traced here: 24.7 us
  Pallas kernels  24.1 us (97%)
  between operations  0.64 us (3%)
    pallas_call x1, Pallas kernels, body(): pl.pallas_call(functools.partial(kernel, n, groups), out_shape=tuple((plt...  23.4 us
    pallas_call x1, Pallas kernels, body(): pl.pallas_call(store_kernel, out_shape=tuple((jax.ShapeDtypeStruct(shape,...  0.68 us

profile of v3, /device:TPU:0, one launch (start us, length us, event | category | flops | bytes accessed | tf_op | source)
XLA Modules:
  0.0 24.7 jit_solution(16502252389044471546)
XLA Ops:
  0.6 23.4 %shard_map.93 = (bf16[1,3,8,1024]{3,2,1,0:T(8,128)(2,1)S(1)}, bf16[1,3,16,256]{3,2,1,0:T(8,128)(2,1)S(1)}, bf16[1,3,16,256]{3,2,1,0:T(8,128)(2,1)S(1)}, bf16[1,3,16,256]{3,2,1,0:T(8,128)(2,1)S(1)}) custom-call(bf16[1,3,16,256]{3,2,1,0:T(8,128)(2,1)} %q_hbm.1, bf16[1,3,16,256]{3,2,1,0:T(8,128)(2,1)} %k_hbm.1, bf16[1,3,16,256]{3,2,1,0:T(8,128)(2,1)} %v_hbm.1, ...), custom_call_target="tpu_custom_call" | custom-call | tf_op jit(solution)/shard_map/pallas_call | solution.py:394
  24.0 0.7 %shard_map.94 = (bf16[1,3,8,1024]{3,2,1,0:T(8,128)(2,1)}, bf16[1,3,16,256]{3,2,1,0:T(8,128)(2,1)}, bf16[1,3,16,256]{3,2,1,0:T(8,128)(2,1)}, bf16[1,3,16,256]{3,2,1,0:T(8,128)(2,1)}) custom-call(bf16[1,3,8,1024]{3,2,1,0:T(8,128)(2,1)S(1)} %get-tuple-element.8.refs_0_, bf16[1,3,16,256]{3,2,1,0:T(8,128)(2,1)S(1)} %get-tuple-element.9.refs_1_, ...), custom_call_target="tpu_custom_call" | custom-call | tf_op jit(solution)/shard_map/pallas_call | solution.py:417
